TPU v7x, 32 devices: a whole 2x2x4 slice. The times are simulated.
32 devices in a mesh: grp: 2 (over y), pos: 16 (over z, x, core).
Axes of the slice: x: 2, y: 2, z: 4, core: 2. Of those that a mesh axis runs over, the one named last changes fastest.
Arguments:
- object_field: float32 [2, 2048, 2048], P(None, 'grp', 'pos'), may hold values from -5 to 5
- probe_field: float32 [2, 256, 256], replicated, may hold values from -5 to 5
- patterns: float32 [96, 256, 256], P(('grp', 'pos')), may hold values from 0.05 to 5
- corners: int32 [2, 96], P(None, ('grp', 'pos')), may hold values from 0 to 1792, as said below
- counts: int32 [32], replicated, may hold values from 1 to 3, as said below
Outputs:
- object_new: float32 [2, 2048, 2048], P(None, 'grp', 'pos')
- probe_new: float32 [2, 256, 256], replicated
Inputs may be any that keep to these rules, and one draw needn't show every extreme that they name: `corners`: each slot's patch of 256 x 256 cells lies inside the object and inside its device's block of 1024 x 128 object cells extended by 128 cells on every side (the device at grp index a and pos index b holds rows a * 1024 to a * 1024 + 1023 and columns b * 128 to b * 128 + 127). The live slots of a device are its first counts[d] slots; some device has all 3 slots live.
All inputs are finite; a program needn't handle non-finite values.
Results may differ from a plain program's by a relative error of at most 0.00012.
Values sent between devices are 32-bit elements; how exact they have to be, the bound alone decides.
A program may use at most 64 MiB of HBM per device.

v0:
```python
import math
import jax
import jax.numpy as jnp
from jax import lax
from jax.sharding import PartitionSpec as P

M = 256
HALO = 128
step_object = 0.25
step_probe = 4.0


def padded(x, sides, width):
    for axis, dim in sides:
        peers, length = (lax.axis_size(axis), x.shape[dim])
        up = [(i, (i + 1) % peers) for i in range(peers - 1)]
        down = [(j, i) for i, j in up]
        last = lax.slice_in_dim(x, length - width, length, axis=dim)
        initial = lax.slice_in_dim(x, 0, width, axis=dim)
        before = lax.ppermute(last, axis, up)
        after = lax.ppermute(initial, axis, down)
        x = jnp.concatenate([before, x, after], axis=dim)
    return x


def product(left, right):
    return jnp.dot(left, right, precision=lax.Precision.HIGHEST, preferred_element_type=jnp.float32)


def left_mul(cos_part, sin_part, real_part, imag_part):
    return (
        product(cos_part, real_part) - product(sin_part, imag_part),
        product(cos_part, imag_part) + product(sin_part, real_part),
    )


def right_mul(real_part, imag_part, cos_part, sin_part):
    return (
        product(real_part, cos_part) - product(imag_part, sin_part),
        product(real_part, sin_part) + product(imag_part, cos_part),
    )


def dft_tables(order):
    indices = jnp.arange(order, dtype=jnp.int32)
    phases = indices[:, None] * indices[None, :] % order
    angles = phases.astype(jnp.float32) * (2.0 * math.pi / order)
    factor = 1.0 / math.sqrt(order)
    return (jnp.cos(angles) * factor, -jnp.sin(angles) * factor)


def far_field(wave, measured, cos_table, sin_table):
    front_re, front_im = left_mul(cos_table, sin_table, wave[0], wave[1])
    far_re, far_im = right_mul(front_re, front_im, cos_table, sin_table)
    excess = far_re * far_re + far_im * far_im - measured
    back_re, back_im = left_mul(cos_table, -sin_table, excess * far_re, excess * far_im)
    chi_re, chi_im = right_mul(back_re, back_im, cos_table, -sin_table)
    return jnp.stack((chi_re, chi_im))


def on_device(object_field, probe_field, patterns, corners, counts):
    tile_rows = object_field.shape[1]
    tile_cols = object_field.shape[2]
    slot_count = patterns.shape[0]
    pos_count = lax.axis_size("pos")
    grp_index = lax.axis_index("grp")
    pos_index = lax.axis_index("pos")
    device = grp_index * pos_count + pos_index
    own_count = counts[device]
    cos_table, sin_table = dft_tables(M)
    extended = padded(object_field, (("grp", 1), ("pos", 2)), HALO)
    row_local = corners[0] - grp_index * tile_rows + HALO
    col_local = corners[1] - pos_index * tile_cols + HALO

    def cut_patch(row_at, col_at):
        return lax.dynamic_slice(extended, (jnp.int32(0), row_at, col_at), (2, M, M))

    patches = jax.vmap(cut_patch)(row_local, col_local)
    waves = jnp.stack(
        (
            probe_field[0] * patches[:, 0] - probe_field[1] * patches[:, 1],
            probe_field[0] * patches[:, 1] + probe_field[1] * patches[:, 0],
        ),
        axis=1,
    )
    empty_results = jnp.zeros((slot_count, 2, M, M), jnp.float32)

    def solve_own(step, results):
        result = far_field(waves[step], patterns[step], cos_table, sin_table)
        return lax.dynamic_update_index_in_dim(results, result, step, 0)

    residuals = lax.fori_loop(0, own_count, solve_own, empty_results)

    def accumulate(step, totals):
        grad_ext, grad_probe = totals
        chi_re = residuals[step, 0]
        chi_im = residuals[step, 1]
        patch_re = patches[step, 0]
        patch_im = patches[step, 1]
        obj_part = jnp.stack(
            (
                probe_field[0] * chi_re + probe_field[1] * chi_im,
                probe_field[0] * chi_im - probe_field[1] * chi_re,
            )
        )
        prb_part = jnp.stack(
            (patch_re * chi_re + patch_im * chi_im, patch_re * chi_im - patch_im * chi_re)
        )
        anchor = (jnp.int32(0), row_local[step], col_local[step])
        current = lax.dynamic_slice(grad_ext, anchor, (2, M, M))
        grad_ext = lax.dynamic_update_slice(grad_ext, current + obj_part, anchor)
        return (grad_ext, grad_probe + prb_part)

    start_totals = (
        jnp.zeros(extended.shape, jnp.float32),
        jnp.zeros(probe_field.shape, jnp.float32),
    )
    grad_ext, grad_probe = lax.fori_loop(0, own_count, accumulate, start_totals)
    col_rims = jnp.concatenate((grad_ext[:, :, :HALO], grad_ext[:, :, -HALO:]), axis=2)
    col_arrived = padded(col_rims, (("pos", 2),), HALO)
    middle = grad_ext[:, :, HALO : HALO + tile_cols]
    middle = middle.at[:, :, :HALO].add(col_arrived[:, :, :HALO])
    middle = middle.at[:, :, tile_cols - HALO :].add(col_arrived[:, :, -HALO:])
    row_rims = jnp.concatenate((middle[:, :HALO], middle[:, -HALO:]), axis=1)
    row_arrived = padded(row_rims, (("grp", 1),), HALO)
    core = middle[:, HALO : HALO + tile_rows]
    core = core.at[:, :HALO].add(row_arrived[:, :HALO])
    core = core.at[:, tile_rows - HALO :].add(row_arrived[:, -HALO:])
    object_new = object_field - step_object * core
    live_total = jnp.sum(counts).astype(jnp.float32)
    share = lax.psum_scatter(grad_probe, "pos", scatter_dimension=1, tiled=True)
    share = lax.psum(share, "grp")
    row_share = M // pos_count
    mine = lax.dynamic_slice_in_dim(probe_field, pos_index * row_share, row_share, 1)
    new_rows = mine - step_probe * share / live_total
    probe_new = lax.all_gather(new_rows, "pos", axis=1, tiled=True)
    return (object_new, probe_new)


def solution(mesh):
    return jax.shard_map(
        on_device,
        mesh=mesh,
        in_specs=(
            P(None, "grp", "pos"),
            P(),
            P(("grp", "pos"), None, None),
            P(None, ("grp", "pos")),
            P(),
        ),
        out_specs=(P(None, "grp", "pos"), P()),
        check_vma=False,
    )
```

profile of v0, /device:TPU:0, one launch (start us, length us, event | category | flops | bytes accessed | tf_op | source)
XLA Modules:
  0.0 322.7 jit_solution(2919764576730867751)
XLA Ops:
  8.3 4.9 %collective-permute-start = (f32[2,128,128]{2,1,0:T(8,128)S(1)}, f32[2,128,128]{2,1,0:T(8,128)S(1)}, u32[]{:S(2)}, u32[]{:S(2)}) collective-permute-start(f32[2,128,128]{2,1,0:T(8,128)S(1)} %get-tuple-element.348), channel_id=1, source_target_pairs={{0,16},{1,17},{2,18},{3,19},{4,20},{5,21},{6,22},{7,23},{8,24},{9,... | collective-permute-start | bytes 393224 | tf_op jit(solution)/shard_map/ppermute | solution.py:20
  13.2 1.3 collective-permute-start.1
  14.5 1.4 collective-permute-done
  15.9 1.3 constant_dynamic-update-slice_fusion.1
  17.2 2.8 collective-permute-done.1
  20.1 1.4 collective-permute-start.2
  21.5 1.3 collective-permute-start.3
  24.4 3.7 %collective-permute-done.3 = f32[2,1280,128]{2,1,0:T(8,128)} collective-permute-done((f32[2,1280,128]{2,1,0:T(8,128)S(1)}, f32[2,1280,128]{2,1,0:T(8,128)}, u32[]{:S(2)}, u32[]{:S(2)}) %collective-permute-start.3) | collective-permute-done | bytes 1310752 | tf_op jit(solution)/shard_map/ppermute | solution.py:21
  28.2 3.4 %pad_maximum_fusion = f32[2,1280,384]{2,1,0:T(8,128)} fusion(f32[2,1280,128]{2,1,0:T(8,128)} %collective-permute-done.3, f32[2,1280,128]{2,1,0:T(8,128)S(1)} %constant_dynamic-update-slice_fusion, f32[2,1280,128]{2,1,0:T(8,128)S(1)} %collective-permute-done.2), kind=kLoop, calls=%fused_computation.139 | loop fusion | flops 1966080 | bytes 7864320 | tf_op jit(solution)/shard_map/concatenate | solution.py:22
  31.8 9.6 %while.33 = (s32[]{:T(128)}, f32[2,1280,384]{2,1,0:T(8,128)}, s32[3,3]{1,0:T(4,128)S(1)}, f32[3,2,256,256]{3,2,1,0:T(8,128)S(1)}, s32[]{:T(128)}) while((s32[]{:T(128)}, f32[2,1280,384]{2,1,0:T(8,128)}, s32[3,3]{1,0:T(4,128)S(1)}, f32[3,2,256,256]{3,2,1,0:T(8,128)S(1)}, s32[]{:T(128)}) %tuple.101), condition=%wide.while_cond.4, body=%wide.while_body.4.sunk | while | flops 2 | bytes 1048693 | solution.py:76
  32.4 2.5 bitcast_dynamic-update-slice_fusion.2
  35.7 2.5 bitcast_dynamic-update-slice_fusion.2
  38.9 2.5 bitcast_dynamic-update-slice_fusion.2
  41.6 1.3 pad_maximum_fusion.1
  42.9 1.3 broadcast_in_dim.20
  44.2 30.9 %while.34 = (s32[]{:T(128)}, f32[3,2,256,256]{3,2,1,0:T(8,128)}, s32[]{:T(128)}, f32[3,2,256,256]{3,2,1,0:T(8,128)}, f32[3,256,256]{2,1,0:T(8,128)}, /*index=5*/s32[]{:T(128)}, s32[]{:T(128)}, s32[]{:T(128)}, s32[]{}) while((s32[]{:T(128)}, f32[3,2,256,256]{3,2,1,0:T(8,128)}, s32[]{:T(128)}, ...), condition=%wide.region_1.2_spmd.clone.clone, body=%wide.region_0.1_spmd.clone.clone.sunk | while | flops 3238789120 | bytes 12320939 | solution.py:92
  44.9 2.4 fusion.179
  47.3 2.4 convolution_subtract_fusion.7
  49.8 1.5 fusion.180
  51.2 2.4 fusion.181
  53.7 2.4 convolution_add_fusion.6
  56.1 1.5 convolution_subtract_fusion.8
  57.6 1.5 fusion.182
  59.1 2.4 fusion.183
  61.5 1.5 fusion.186
  63.0 1.5 convolution_add_fusion.7
  64.5 1.5 fusion.184
  66.0 1.5 convolution_subtract_fusion.9
  67.5 1.5 fusion.188
  68.9 1.5 fusion.189
  70.4 1.5 fusion.185
  71.9 1.5 fusion.187
  75.1 2.1 broadcast_in_dim.18
  77.3 14.2 %while.32 = (s32[]{:T(128)}, f32[2,1280,384]{2,1,0:T(8,128)}, f32[2,256,256]{2,1,0:T(8,128)S(1)}, s32[]{:T(128)}, s32[3]{0:T(128)S(1)}, /*index=5*/s32[3]{0:T(12...) while((s32[]{:T(128)}, f32[2,1280,384]{2,1,0:T(8,128)}, ...), condition=%wide.region_3.4_spmd, body=%wide.region_2.3_spmd.sunk | while | flops 1310731 | bytes 6816019 | solution.py:118
  83.1 1.1 fusion.161
  84.2 1.4 maximum_add_fusion.3
  85.6 5.2 %dynamic_update_slice.13 = f32[2,1280,384]{2,1,0:T(8,128)} dynamic-update-slice(f32[2,1280,384]{2,1,0:T(8,128)} %get-tuple-element.545, f32[2,256,256]{2,1,0:T(8,128)S(1)} %get-tuple-element.473, s32[]{:T(128)} %constant.180.clone.1..sunk, s32[]{:T(128)S(6)} %select_n.163, s32[]{:T(128)S(6)} %select_n.164) | dynamic-update-slice | bytes 1048580 | tf_op jit(solution)/shard_map/while/body/dynamic_update_slice | solution.py:111
  91.5 3.2 fusion.116
  94.7 27.6 %collective-permute-start.4 = (f32[2,1280,128]{2,1,0:T(8,128)}, f32[2,1280,128]{2,1,0:T(8,128)S(1)}, u32[]{:S(2)}, u32[]{:S(2)}) collective-permute-start(f32[2,1280,128]{2,1,0:T(8,128)} %get-tuple-element.341), channel_id=1, source_target_pairs={{0,1},{1,2},{2,3},{3,4},{4,5},{5,6},{6,7},{7,8},{8,9},{9,10},{10,1... | collective-permute-start | bytes 3932168 | tf_op jit(solution)/shard_map/ppermute | solution.py:20
  122.3 1.3 collective-permute-start.5
  124.9 147.0 %reduce-scatter.2.cloned.1.call-done = f32[2,16,256]{2,1,0:T(8,128)} async-done(((f32[2,256,256]{2,1,0:T(8,128)}), f32[2,16,256]{2,1,0:T(8,128)}) %reduce-scatter.2.cloned.1.call-update) | async-done | bytes 32784 | tf_op jit(solution)/shard_map/reduce_scatter | solution.py:131
  271.9 9.0 %psum.7 = f32[2,16,256]{2,1,0:T(8,128)S(1)} all-reduce(f32[2,16,256]{2,1,0:T(8,128)} %reduce-scatter.2.cloned.1.call-done), channel_id=1, replica_groups=mesh['grp'=2,'pos'=16] {'grp'}, use_global_device_ids=true, to_apply=%region_5.6 | all-reduce | flops 8192 | bytes 65536 | tf_op jit(solution)/shard_map/psum | solution.py:132
  280.9 1.9 add_add_fusion
  282.8 2.5 collective-permute-start.6
  285.3 20.9 %all_gather.3 = f32[2,256,256]{2,1,0:T(8,128)S(1)} all-gather(f32[2,16,256]{2,1,0:T(8,128)S(1)} %divide_subtract_fusion), channel_id=1, replica_groups=mesh['grp'=2,'pos'=16] {'pos'}, dimensions={1}, use_global_device_ids=true | all-gather | bytes 557056 | tf_op jit(solution)/shard_map/all_gather | solution.py:136
  306.2 1.4 collective-permute-start.7
  307.7 6.3 %collective-permute-done.7 = f32[2,128,128]{2,1,0:T(8,128)S(1)} collective-permute-done((f32[2,128,128]{2,1,0:T(8,128)S(1)}, f32[2,128,128]{2,1,0:T(8,128)S(1)}, u32[]{:S(2)}, u32[]{:S(2)}) %collective-permute-start.7) | collective-permute-done | bytes 131104 | tf_op jit(solution)/shard_map/ppermute | solution.py:21
  314.0 1.1 multiply_subtract_fusion
  (49 shorter events, 8.7 us)
Async XLA Ops:
  7.2 15.6 %copy-start.5 = (s32[2,3]{1,0:T(2,128)S(1)}, s32[2,3]{1,0:T(2,128)}, u32[]{:S(2)}) copy-start(s32[2,3]{1,0:T(2,128)} %param.24) | copy-start | bytes 76
  7.2 15.7 %copy-start.6 = (s32[32]{0:T(128)S(1)}, s32[32]{0:T(128)}, u32[]{:S(2)}) copy-start(s32[32]{0:T(128)} %param.25) | copy-start | bytes 388
  7.2 16.4 %copy-start.1 = (f32[2,256,256]{2,1,0:T(8,128)S(1)}, f32[2,256,256]{2,1,0:T(8,128)}, u32[]{:S(2)}) copy-start(f32[2,256,256]{2,1,0:T(8,128)} %param.22) | copy-start | bytes 1572868
  7.2 264.7 %reduce-scatter.2.cloned.1.call-start = ((), (), s32[]{:S(2)}) async-start(), calls=%async_computation.1 | async-start | bytes 557056 | tf_op jit(solution)/shard_map/reduce_scatter | solution.py:131
  8.3 7.6 %collective-permute-start = (f32[2,128,128]{2,1,0:T(8,128)S(1)}, f32[2,128,128]{2,1,0:T(8,128)S(1)}, u32[]{:S(2)}, u32[]{:S(2)}) collective-permute-start(f32[2,128,128]{2,1,0:T(8,128)S(1)} %get-tuple-element.348), channel_id=1, source_target_pairs={{0,16},{1,17},{2,18},{3,19},{4,20},{5,21},{6,22},{7,23},{8,24},{9,... | collective-permute-start | bytes 393224 | tf_op jit(solution)/shard_map/ppermute | solution.py:20
  13.2 6.9 %collective-permute-start.1 = (f32[2,128,128]{2,1,0:T(8,128)S(1)}, f32[2,128,128]{2,1,0:T(8,128)S(1)}, u32[]{:S(2)}, u32[]{:S(2)}) collective-permute-start(f32[2,128,128]{2,1,0:T(8,128)S(1)} %get-tuple-element.347), channel_id=1, source_target_pairs={{16,0},{17,1},{18,2},{19,3},{20,4},{21,5},{22,6},{23,7},{24,8},{25... | collective-permute-start | bytes 393224 | tf_op jit(solution)/shard_map/ppermute | solution.py:21
  20.1 4.3 %collective-permute-start.2 = (f32[2,1280,128]{2,1,0:T(8,128)S(1)}, f32[2,1280,128]{2,1,0:T(8,128)S(1)}, u32[]{:S(2)}, u32[]{:S(2)}) collective-permute-start(f32[2,1280,128]{2,1,0:T(8,128)S(1)} %constant_dynamic-update-slice_fusion), channel_id=1, source_target_pairs={{0,1},{1,2},{2,3},{3,4},{4,5},{5,6},{6,7},{7,8},{8,9},{9,10},{10,1... | collective-permute-start | bytes 3932168 | tf_op jit(solution)/shard_map/ppermute | solution.py:20
  21.5 6.7 %collective-permute-start.3 = (f32[2,1280,128]{2,1,0:T(8,128)S(1)}, f32[2,1280,128]{2,1,0:T(8,128)}, u32[]{:S(2)}, u32[]{:S(2)}) collective-permute-start(f32[2,1280,128]{2,1,0:T(8,128)S(1)} %constant_dynamic-update-slice_fusion), channel_id=1, source_target_pairs={{1,0},{2,1},{3,2},{4,3},{5,4},{6,5},{7,6},{8,7},{9,8},{10,9},{11,1... | collective-permute-start | bytes 3932168 | tf_op jit(solution)/shard_map/ppermute | solution.py:21
  31.7 9.7 %copy-start.3 = (f32[256,256]{1,0:T(8,128)S(1)}, f32[256,256]{1,0:T(8,128)}, u32[]{:S(2)}) copy-start(f32[256,256]{1,0:T(8,128)} %get-tuple-element.349) | copy-start | bytes 786436
  31.7 9.7 %copy-start.4 = (f32[256,256]{1,0:T(8,128)S(1)}, f32[256,256]{1,0:T(8,128)}, u32[]{:S(2)}) copy-start(f32[256,256]{1,0:T(8,128)} %get-tuple-element.350) | copy-start | bytes 786436
  91.5 3.2 copy-start
  94.7 186.2 %collective-permute-start.4 = (f32[2,1280,128]{2,1,0:T(8,128)}, f32[2,1280,128]{2,1,0:T(8,128)S(1)}, u32[]{:S(2)}, u32[]{:S(2)}) collective-permute-start(f32[2,1280,128]{2,1,0:T(8,128)} %get-tuple-element.341), channel_id=1, source_target_pairs={{0,1},{1,2},{2,3},{3,4},{4,5},{5,6},{6,7},{7,8},{8,9},{9,10},{10,1... | collective-permute-start | bytes 3932168 | tf_op jit(solution)/shard_map/ppermute | solution.py:20
  122.3 158.6 %collective-permute-start.5 = (f32[2,1280,128]{2,1,0:T(8,128)S(1)}, f32[2,1280,128]{2,1,0:T(8,128)}, u32[]{:S(2)}, u32[]{:S(2)}) collective-permute-start(f32[2,1280,128]{2,1,0:T(8,128)S(1)} %get-tuple-element.342), channel_id=1, source_target_pairs={{1,0},{2,1},{3,2},{4,3},{5,4},{6,5},{7,6},{8,7},{9,8},{10,9},{11,1... | collective-permute-start | bytes 3932168 | tf_op jit(solution)/shard_map/ppermute | solution.py:21
  282.8 24.8 %collective-permute-start.6 = (f32[2,128,128]{2,1,0:T(8,128)S(1)}, f32[2,128,128]{2,1,0:T(8,128)S(1)}, u32[]{:S(2)}, u32[]{:S(2)}) collective-permute-start(f32[2,128,128]{2,1,0:T(8,128)S(1)} %get-tuple-element.346), channel_id=1, source_target_pairs={{0,16},{1,17},{2,18},{3,19},{4,20},{5,21},{6,22},{7,23},{8,24},{9,... | collective-permute-start | bytes 393224 | tf_op jit(solution)/shard_map/ppermute | solution.py:20
  306.1 7.9 %copy-start.2 = (f32[2,1024,128]{2,1,0:T(8,128)S(1)}, f32[2,1024,128]{2,1,0:T(8,128)}, u32[]{:S(2)}) copy-start(f32[2,1024,128]{2,1,0:T(8,128)} %param.21) | copy-start | bytes 3145732
  306.2 7.8 %collective-permute-start.7 = (f32[2,128,128]{2,1,0:T(8,128)S(1)}, f32[2,128,128]{2,1,0:T(8,128)S(1)}, u32[]{:S(2)}, u32[]{:S(2)}) collective-permute-start(f32[2,128,128]{2,1,0:T(8,128)S(1)} %get-tuple-element.345), channel_id=1, source_target_pairs={{16,0},{17,1},{18,2},{19,3},{20,4},{21,5},{22,6},{23,7},{24,8},{25... | collective-permute-start | bytes 393224 | tf_op jit(solution)/shard_map/ppermute | solution.py:21
Sparse Core Ops, SparseCore 0:
  123.8 148.0 reduce-scatter.1
where the time goes:
time: 325 us; the launch traced here: 323 us
  waiting for transfers between devices  161 us (50%)
  starting transfers between devices  41.7 us (13%)
  blocking collectives  29.8 us (9%)
  matrix products  28.4 us (9%)
  local copies, waits for them, and re-layouts  27.6 us (8%)
  between operations  15 us (5%)
  other arithmetic  11.9 us (4%)
  loops' own time  7.08 us (2%)
    reduce_scatter x1, waiting for transfers between devices, on_device(): share = lax.psum_scatter(grad_probe, 'pos', scatter_dimension=1, tiled=True)  147 us
    ppermute x4, starting transfers between devices, padded(): before = lax.ppermute(last, axis, up)  36.3 us
    dot_general x16, matrix products, product(): jnp.dot(left, right, precision=lax.Precision.HIGHEST, preferred_element_t...  28.4 us
    all_gather x1, blocking collectives, on_device(): probe_new = lax.all_gather(new_rows, 'pos', axis=1, tiled=True)  20.9 us
    ppermute x4, waiting for transfers between devices, padded(): after = lax.ppermute(initial, axis, down)  12.9 us
    gather x9, local copies, waits for them, and re-layouts  9.58 us
    psum x1, blocking collectives, on_device(): share = lax.psum(share, 'grp')  8.97 us
  transfers between devices with their start and end apart: 9, of which 5 were waited for; matrix products, arithmetic and copies ran while one was open for 1% of the time, Pallas kernels for 0%

commit v1 on v0

--- a/solution.py
+++ b/solution.py
@@ -133,7 +133,7 @@
     row_share = M // pos_count
     mine = lax.dynamic_slice_in_dim(probe_field, pos_index * row_share, row_share, 1)
     new_rows = mine - step_probe * share / live_total
-    probe_new = lax.all_gather(new_rows, "pos", axis=1, tiled=True)
+    probe_new = jnp.concatenate(lax.all_gather(new_rows, "pos"), axis=1)
     return (object_new, probe_new)
 
 

time: 325 us -> 324 us (level)
  no operation moved by 1% of the time
where the time goes in v1:
time: 324 us; the launch traced here: 322 us
  waiting for transfers between devices  161 us (50%)
  starting transfers between devices  41.7 us (13%)
  blocking collectives  29.8 us (9%)
  matrix products  28.3 us (9%)
  local copies, waits for them, and re-layouts  27.9 us (9%)
  between operations  15 us (5%)
  other arithmetic  11.6 us (4%)
  loops' own time  6.58 us (2%)
    reduce_scatter x1, waiting for transfers between devices, on_device(): share = lax.psum_scatter(grad_probe, 'pos', scatter_dimension=1, tiled=True)  146 us
    ppermute x4, starting transfers between devices, padded(): before = lax.ppermute(last, axis, up)  36.3 us
    dot_general x16, matrix products, product(): jnp.dot(left, right, precision=lax.Precision.HIGHEST, preferred_element_t...  28.3 us
    all_gather x1, blocking collectives, on_device(): probe_new = jnp.concatenate(lax.all_gather(new_rows, 'pos'), axis=1)  20.9 us
    ppermute x4, waiting for transfers between devices, padded(): after = lax.ppermute(initial, axis, down)  13 us
    gather x9, local copies, waits for them, and re-layouts  9.57 us
    psum x1, blocking collectives, on_device(): share = lax.psum(share, 'grp')  8.96 us
  transfers between devices with their start and end apart: 9, of which 5 were waited for; matrix products, arithmetic and copies ran while one was open for 1% of the time, Pallas kernels for 0%

profile of v1, /device:TPU:0, one launch (start us, length us, event | category | flops | bytes accessed | tf_op | source)
XLA Modules:
  0.0 321.5 jit_solution(2601166564011665974)
XLA Ops:
  8.3 4.9 %collective-permute-start = (f32[2,128,128]{2,1,0:T(8,128)S(1)}, f32[2,128,128]{2,1,0:T(8,128)S(1)}, u32[]{:S(2)}, u32[]{:S(2)}) collective-permute-start(f32[2,128,128]{2,1,0:T(8,128)S(1)} %get-tuple-element.352), channel_id=1, source_target_pairs={{0,16},{1,17},{2,18},{3,19},{4,20},{5,21},{6,22},{7,23},{8,24},{9,... | collective-permute-start | bytes 393224 | tf_op jit(solution)/shard_map/ppermute | solution.py:20
  13.2 1.3 collective-permute-start.1
  14.5 1.4 collective-permute-done
  15.9 1.3 constant_dynamic-update-slice_fusion.1
  17.2 2.8 collective-permute-done.1
  20.1 1.4 collective-permute-start.2
  21.5 1.3 collective-permute-start.3
  24.2 3.9 %collective-permute-done.3 = f32[2,1280,128]{2,1,0:T(8,128)} collective-permute-done((f32[2,1280,128]{2,1,0:T(8,128)S(1)}, f32[2,1280,128]{2,1,0:T(8,128)}, u32[]{:S(2)}, u32[]{:S(2)}) %collective-permute-start.3) | collective-permute-done | bytes 1310752 | tf_op jit(solution)/shard_map/ppermute | solution.py:21
  28.2 3.4 %pad_maximum_fusion = f32[2,1280,384]{2,1,0:T(8,128)} fusion(f32[2,1280,128]{2,1,0:T(8,128)} %collective-permute-done.3, f32[2,1280,128]{2,1,0:T(8,128)S(1)} %constant_dynamic-update-slice_fusion, f32[2,1280,128]{2,1,0:T(8,128)S(1)} %collective-permute-done.2), kind=kLoop, calls=%fused_computation.139 | loop fusion | flops 1966080 | bytes 7864320 | tf_op jit(solution)/shard_map/concatenate | solution.py:22
  31.7 9.6 %while.33 = (s32[]{:T(128)}, f32[2,1280,384]{2,1,0:T(8,128)}, s32[3,3]{1,0:T(4,128)S(1)}, f32[3,2,256,256]{3,2,1,0:T(8,128)S(1)}, s32[]{:T(128)}) while((s32[]{:T(128)}, f32[2,1280,384]{2,1,0:T(8,128)}, s32[3,3]{1,0:T(4,128)S(1)}, f32[3,2,256,256]{3,2,1,0:T(8,128)S(1)}, s32[]{:T(128)}) %tuple.102), condition=%wide.while_cond.4, body=%wide.while_body.4.sunk | while | flops 2 | bytes 1048693 | solution.py:76
  32.4 2.5 bitcast_dynamic-update-slice_fusion.2
  35.6 2.5 bitcast_dynamic-update-slice_fusion.2
  38.9 2.5 bitcast_dynamic-update-slice_fusion.2
  41.6 1.3 pad_maximum_fusion.1
  42.8 1.3 broadcast_in_dim.20
  44.2 30.6 %while.34 = (s32[]{:T(128)}, f32[3,2,256,256]{3,2,1,0:T(8,128)}, s32[]{:T(128)}, f32[3,2,256,256]{3,2,1,0:T(8,128)}, f32[3,256,256]{2,1,0:T(8,128)}, /*index=5*/s32[]{:T(128)}, s32[]{:T(128)}, s32[]{:T(128)}, s32[]{}) while((s32[]{:T(128)}, f32[3,2,256,256]{3,2,1,0:T(8,128)}, s32[]{:T(128)}, ...), condition=%wide.region_1.2_spmd.clone.clone, body=%wide.region_0.1_spmd.clone.clone.sunk | while | flops 3238789120 | bytes 12320939 | solution.py:92
  44.7 2.4 fusion.179
  47.2 2.4 convolution_subtract_fusion.7
  49.6 1.5 fusion.180
  51.1 2.4 fusion.181
  53.5 2.4 convolution_add_fusion.6
  56.0 1.5 convolution_subtract_fusion.8
  57.4 1.5 fusion.182
  58.9 2.4 fusion.183
  61.3 1.5 fusion.186
  62.8 1.5 convolution_add_fusion.7
  64.3 1.5 fusion.184
  65.8 1.5 convolution_subtract_fusion.9
  67.3 1.5 fusion.188
  68.7 1.5 fusion.189
  70.2 1.5 fusion.185
  71.7 1.5 fusion.187
  74.8 2.1 broadcast_in_dim.18
  76.9 14.0 %while.32 = (s32[]{:T(128)}, f32[2,1280,384]{2,1,0:T(8,128)}, f32[2,256,256]{2,1,0:T(8,128)S(1)}, s32[]{:T(128)}, s32[3]{0:T(128)S(1)}, /*index=5*/s32[3]{0:T(12...) while((s32[]{:T(128)}, f32[2,1280,384]{2,1,0:T(8,128)}, ...), condition=%wide.region_3.4_spmd, body=%wide.region_2.3_spmd.sunk | while | flops 1310731 | bytes 6816019 | solution.py:118
  82.6 1.1 fusion.161
  83.7 1.4 maximum_add_fusion.3
  85.1 5.2 %dynamic_update_slice.13 = f32[2,1280,384]{2,1,0:T(8,128)} dynamic-update-slice(f32[2,1280,384]{2,1,0:T(8,128)} %get-tuple-element.549, f32[2,256,256]{2,1,0:T(8,128)S(1)} %get-tuple-element.477, s32[]{:T(128)} %constant.180.clone.1..sunk, s32[]{:T(128)S(6)} %select_n.163, s32[]{:T(128)S(6)} %select_n.164) | dynamic-update-slice | bytes 1048580 | tf_op jit(solution)/shard_map/while/body/dynamic_update_slice | solution.py:111
  90.9 3.6 %fusion.116 = (f32[2,1280,128]{2,1,0:T(8,128)}, f32[2,1280,128]{2,1,0:T(8,128)}) fusion(f32[2,1280,384]{2,1,0:T(8,128)} %get-tuple-element.227), kind=kLoop, calls=%fused_computation.163 | loop fusion | bytes 5242880 | tf_op jit(solution)/shard_map/slice | solution.py:119
  94.5 27.6 %collective-permute-start.4 = (f32[2,1280,128]{2,1,0:T(8,128)}, f32[2,1280,128]{2,1,0:T(8,128)S(1)}, u32[]{:S(2)}, u32[]{:S(2)}) collective-permute-start(f32[2,1280,128]{2,1,0:T(8,128)} %get-tuple-element.345), channel_id=1, source_target_pairs={{0,1},{1,2},{2,3},{3,4},{4,5},{5,6},{6,7},{7,8},{8,9},{9,10},{10,1... | collective-permute-start | bytes 3932168 | tf_op jit(solution)/shard_map/ppermute | solution.py:20
  122.1 1.3 collective-permute-start.5
  124.8 146.3 %reduce-scatter.2.cloned.1.call-done = f32[2,16,256]{2,1,0:T(8,128)} async-done(((f32[2,256,256]{2,1,0:T(8,128)}), f32[2,16,256]{2,1,0:T(8,128)}) %reduce-scatter.2.cloned.1.call-update) | async-done | bytes 32784 | tf_op jit(solution)/shard_map/reduce_scatter | solution.py:131
  271.0 9.0 %psum.7 = f32[2,16,256]{2,1,0:T(8,128)S(1)} all-reduce(f32[2,16,256]{2,1,0:T(8,128)} %reduce-scatter.2.cloned.1.call-done), channel_id=1, replica_groups=mesh['grp'=2,'pos'=16] {'grp'}, use_global_device_ids=true, to_apply=%region_5.6 | all-reduce | flops 8192 | bytes 65536 | tf_op jit(solution)/shard_map/psum | solution.py:132
  280.0 1.5 add_add_fusion
  281.6 2.5 collective-permute-start.6
  284.0 20.9 %all-gather = f32[32,16,256]{2,1,0:T(8,128)S(1)} all-gather(f32[2,16,256]{2,1,0:T(8,128)S(1)} %divide_subtract_fusion), channel_id=2, replica_groups=mesh['grp'=2,'pos'=16] {'pos'}, dimensions={0}, use_global_device_ids=true | all-gather | bytes 557056 | tf_op jit(solution)/shard_map/all_gather | solution.py:136
  305.8 1.4 collective-permute-start.7
  307.3 6.3 %collective-permute-done.7 = f32[2,128,128]{2,1,0:T(8,128)S(1)} collective-permute-done((f32[2,128,128]{2,1,0:T(8,128)S(1)}, f32[2,128,128]{2,1,0:T(8,128)S(1)}, u32[]{:S(2)}, u32[]{:S(2)}) %collective-permute-start.7) | collective-permute-done | bytes 131104 | tf_op jit(solution)/shard_map/ppermute | solution.py:21
  313.6 1.1 multiply_subtract_fusion
  (47 shorter events, 8.6 us)
Async XLA Ops:
  7.2 15.6 %copy-start.4 = (s32[2,3]{1,0:T(2,128)S(1)}, s32[2,3]{1,0:T(2,128)}, u32[]{:S(2)}) copy-start(s32[2,3]{1,0:T(2,128)} %param.24) | copy-start | bytes 76
  7.2 15.7 %copy-start.5 = (s32[32]{0:T(128)S(1)}, s32[32]{0:T(128)}, u32[]{:S(2)}) copy-start(s32[32]{0:T(128)} %param.25) | copy-start | bytes 388
  7.2 16.3 %copy-start.1 = (f32[2,256,256]{2,1,0:T(8,128)S(1)}, f32[2,256,256]{2,1,0:T(8,128)}, u32[]{:S(2)}) copy-start(f32[2,256,256]{2,1,0:T(8,128)} %param.22) | copy-start | bytes 1572868
  7.2 263.8 %reduce-scatter.2.cloned.1.call-start = ((), (), s32[]{:S(2)}) async-start(), calls=%async_computation.1 | async-start | bytes 557056 | tf_op jit(solution)/shard_map/reduce_scatter | solution.py:131
  8.3 7.6 %collective-permute-start = (f32[2,128,128]{2,1,0:T(8,128)S(1)}, f32[2,128,128]{2,1,0:T(8,128)S(1)}, u32[]{:S(2)}, u32[]{:S(2)}) collective-permute-start(f32[2,128,128]{2,1,0:T(8,128)S(1)} %get-tuple-element.352), channel_id=1, source_target_pairs={{0,16},{1,17},{2,18},{3,19},{4,20},{5,21},{6,22},{7,23},{8,24},{9,... | collective-permute-start | bytes 393224 | tf_op jit(solution)/shard_map/ppermute | solution.py:20
  13.2 6.9 %collective-permute-start.1 = (f32[2,128,128]{2,1,0:T(8,128)S(1)}, f32[2,128,128]{2,1,0:T(8,128)S(1)}, u32[]{:S(2)}, u32[]{:S(2)}) collective-permute-start(f32[2,128,128]{2,1,0:T(8,128)S(1)} %get-tuple-element.351), channel_id=1, source_target_pairs={{16,0},{17,1},{18,2},{19,3},{20,4},{21,5},{22,6},{23,7},{24,8},{25... | collective-permute-start | bytes 393224 | tf_op jit(solution)/shard_map/ppermute | solution.py:21
  20.1 4.2 %collective-permute-start.2 = (f32[2,1280,128]{2,1,0:T(8,128)S(1)}, f32[2,1280,128]{2,1,0:T(8,128)S(1)}, u32[]{:S(2)}, u32[]{:S(2)}) collective-permute-start(f32[2,1280,128]{2,1,0:T(8,128)S(1)} %constant_dynamic-update-slice_fusion), channel_id=1, source_target_pairs={{0,1},{1,2},{2,3},{3,4},{4,5},{5,6},{6,7},{7,8},{8,9},{9,10},{10,1... | collective-permute-start | bytes 3932168 | tf_op jit(solution)/shard_map/ppermute | solution.py:20
  21.5 6.7 %collective-permute-start.3 = (f32[2,1280,128]{2,1,0:T(8,128)S(1)}, f32[2,1280,128]{2,1,0:T(8,128)}, u32[]{:S(2)}, u32[]{:S(2)}) collective-permute-start(f32[2,1280,128]{2,1,0:T(8,128)S(1)} %constant_dynamic-update-slice_fusion), channel_id=1, source_target_pairs={{1,0},{2,1},{3,2},{4,3},{5,4},{6,5},{7,6},{8,7},{9,8},{10,9},{11,1... | collective-permute-start | bytes 3932168 | tf_op jit(solution)/shard_map/ppermute | solution.py:21
  31.7 9.7 %copy-start.3 = (f32[256,256]{1,0:T(8,128)S(1)}, f32[256,256]{1,0:T(8,128)}, u32[]{:S(2)}) copy-start(f32[256,256]{1,0:T(8,128)} %get-tuple-element.354) | copy-start | bytes 786436
  90.9 3.6 %copy-start = (f32[2,256,256]{2,1,0:T(8,128)}, f32[2,256,256]{2,1,0:T(8,128)S(1)}, u32[]{:S(2)}) copy-start(f32[2,256,256]{2,1,0:T(8,128)S(1)} %get-tuple-element.228) | copy-start | bytes 1572868
  94.5 185.5 %collective-permute-start.4 = (f32[2,1280,128]{2,1,0:T(8,128)}, f32[2,1280,128]{2,1,0:T(8,128)S(1)}, u32[]{:S(2)}, u32[]{:S(2)}) collective-permute-start(f32[2,1280,128]{2,1,0:T(8,128)} %get-tuple-element.345), channel_id=1, source_target_pairs={{0,1},{1,2},{2,3},{3,4},{4,5},{5,6},{6,7},{7,8},{8,9},{9,10},{10,1... | collective-permute-start | bytes 3932168 | tf_op jit(solution)/shard_map/ppermute | solution.py:20
  122.1 157.9 %collective-permute-start.5 = (f32[2,1280,128]{2,1,0:T(8,128)}, f32[2,1280,128]{2,1,0:T(8,128)S(1)}, u32[]{:S(2)}, u32[]{:S(2)}) collective-permute-start(f32[2,1280,128]{2,1,0:T(8,128)} %get-tuple-element.346), channel_id=1, source_target_pairs={{1,0},{2,1},{3,2},{4,3},{5,4},{6,5},{7,6},{8,7},{9,8},{10,9},{11,1... | collective-permute-start | bytes 3932168 | tf_op jit(solution)/shard_map/ppermute | solution.py:21
  281.6 25.7 %collective-permute-start.6 = (f32[2,128,128]{2,1,0:T(8,128)S(1)}, f32[2,128,128]{2,1,0:T(8,128)S(1)}, u32[]{:S(2)}, u32[]{:S(2)}) collective-permute-start(f32[2,128,128]{2,1,0:T(8,128)S(1)} %get-tuple-element.350), channel_id=1, source_target_pairs={{0,16},{1,17},{2,18},{3,19},{4,20},{5,21},{6,22},{7,23},{8,24},{9,... | collective-permute-start | bytes 393224 | tf_op jit(solution)/shard_map/ppermute | solution.py:20
  305.7 7.9 %copy-start.2 = (f32[2,1024,128]{2,1,0:T(8,128)S(1)}, f32[2,1024,128]{2,1,0:T(8,128)}, u32[]{:S(2)}) copy-start(f32[2,1024,128]{2,1,0:T(8,128)} %param.21) | copy-start | bytes 3145732
  305.8 7.8 %collective-permute-start.7 = (f32[2,128,128]{2,1,0:T(8,128)S(1)}, f32[2,128,128]{2,1,0:T(8,128)S(1)}, u32[]{:S(2)}, u32[]{:S(2)}) collective-permute-start(f32[2,128,128]{2,1,0:T(8,128)S(1)} %get-tuple-element.349), channel_id=1, source_target_pairs={{16,0},{17,1},{18,2},{19,3},{20,4},{21,5},{22,6},{23,7},{24,8},{25... | collective-permute-start | bytes 393224 | tf_op jit(solution)/shard_map/ppermute | solution.py:21
Sparse Core Ops, SparseCore 0:
  123.6 147.3 reduce-scatter.1
